TPU v7x, 32 devices: a whole 2x2x4 slice. The times are simulated.
32 devices in a mesh: dp: 4 (over y, x), tensor: 8 (over z, core).
Axes of the slice: x: 2, y: 2, z: 4, core: 2. Of those that a mesh axis runs over, the one named last changes fastest.
Arguments:
- tokens: bfloat16 [96, 8192], P(('dp', 'tensor')), may hold values from -6 to 6
- weight_store: bfloat16 [2, 192, 128, 128], P(None, 'tensor', 'dp'), may hold values from -0.25 to 0.25
- block_cols: int32 [24, 8], P('tensor'), may hold values from 0 to 63, as said below
- block_count: int32 [24], P('tensor'), may hold values from 1 to 8, 108 in all
- block_home: int32 [8, 24], P('tensor'), may hold values from 0 to 23, each once within a row
- grad_hidden: bfloat16 [96, 3072], P('dp', 'tensor'), may hold values from -6 to 6
Outputs:
- hidden: bfloat16 [96, 3072], P('dp', 'tensor')
- grad_tokens: bfloat16 [96, 8192], P(('dp', 'tensor'))
- grad_weights: bfloat16 [2, 192, 128, 128], P(None, 'tensor', 'dp')
Inputs may be any that keep to these rules, and one draw needn't show every extreme that they name: `block_cols`: the 8 column blocks listed for one hidden block are all different. `block_count`: some hidden block has all 8 slots present. `block_home`: each row is a permutation of 0 to 23.
All inputs are finite; a program needn't handle non-finite values.
Results may differ from a plain program's by a relative error of at most 0.009.
Values may be sent and summed in bfloat16 or wider, within the bound.
A program may use at most 64 MiB of HBM per device.

v0:
```python
import jax
import jax.numpy as jnp
from jax import lax
from jax.sharding import PartitionSpec as P


def body(tokens, weight_store, block_cols, block_count, block_home, grad_hidden):
    rows_here = tokens.shape[0]
    model_width = tokens.shape[1]
    block_size = weight_store.shape[3]
    hidden_blocks, slot_count = block_cols.shape
    all_slots = hidden_blocks * slot_count
    col_blocks = model_width // block_size
    flat_cols = block_cols.reshape(-1)

    def select_blocks(rows):
        shaped = rows.reshape(rows.shape[0], col_blocks, block_size)
        return jnp.take(shaped, flat_cols, axis=1).reshape(
            rows.shape[0], hidden_blocks, slot_count, block_size
        )

    gathered = lax.all_gather(tokens, "tensor", axis=0, tiled=True)
    group_rows = gathered.shape[0]
    blocks = lax.all_gather(weight_store, "dp", axis=2, tiled=True)
    ordered = jnp.take(blocks, block_home[0], axis=1)
    present = (lax.iota(jnp.int32, slot_count)[None, :] < block_count[:, None]).astype(jnp.bfloat16)
    weights = (
        ordered.reshape(2, hidden_blocks, slot_count, block_size, block_size)
        * present[None, :, :, None, None]
    )
    picked = select_blocks(gathered)
    gate_pre = jnp.einsum("thkb,hkbc->thc", picked, weights[0], preferred_element_type=jnp.float32)
    up_pre = jnp.einsum("thkb,hkbc->thc", picked, weights[1], preferred_element_type=jnp.float32)
    gate_sigma = jax.nn.sigmoid(gate_pre)
    activated = gate_pre * gate_sigma
    hidden = (
        (activated * up_pre).astype(jnp.bfloat16).reshape(group_rows, hidden_blocks * block_size)
    )
    grad_in = grad_hidden.reshape(group_rows, hidden_blocks, block_size).astype(jnp.float32)
    grad_gate = (grad_in * up_pre * gate_sigma * (1.0 + gate_pre * (1.0 - gate_sigma))).astype(
        jnp.bfloat16
    )
    grad_up = (grad_in * activated).astype(jnp.bfloat16)
    back_term = jnp.einsum(
        "thc,hkbc->thkb", grad_gate, weights[0], preferred_element_type=jnp.float32
    )
    back_term = back_term + jnp.einsum(
        "thc,hkbc->thkb", grad_up, weights[1], preferred_element_type=jnp.float32
    )
    spread = jnp.zeros((rows_here * lax.axis_size("tensor"), col_blocks, block_size), jnp.float32)
    spread = spread.at[:, flat_cols].add(
        back_term.reshape(rows_here * lax.axis_size("tensor"), all_slots, block_size)
    )
    grad_tokens = lax.psum_scatter(
        spread.reshape(rows_here * lax.axis_size("tensor"), model_width),
        "tensor",
        scatter_dimension=0,
        tiled=True,
    ).astype(jnp.bfloat16)
    fetched = lax.all_gather(tokens, "tensor", axis=0, tiled=True)
    source = select_blocks(fetched)
    part_gate = jnp.einsum("thkb,thc->hkbc", source, grad_gate, preferred_element_type=jnp.float32)
    part_up = jnp.einsum("thkb,thc->hkbc", source, grad_up, preferred_element_type=jnp.float32)
    partial_value = (
        jnp.stack([part_gate, part_up]) * present.astype(jnp.float32)[None, :, :, None, None]
    )
    partial_value = partial_value.reshape(2, all_slots, block_size, block_size)
    grad_store = jnp.zeros_like(partial_value).at[:, block_home[0]].set(partial_value)
    summed = lax.psum_scatter(
        grad_store.astype(jnp.bfloat16), "dp", scatter_dimension=2, tiled=True
    )
    return (hidden, grad_tokens, summed)


def solution(mesh):
    return jax.shard_map(
        body,
        mesh=mesh,
        in_specs=(
            P(("dp", "tensor"), None),
            P(None, "tensor", "dp", None),
            P("tensor", None),
            P("tensor"),
            P("tensor", None),
            P("dp", "tensor"),
        ),
        out_specs=(P("dp", "tensor"), P(("dp", "tensor"), None), P(None, "tensor", "dp", None)),
        check_vma=False,
    )
```

profile of v0, /device:TPU:0, one launch (start us, length us, event | category | flops | bytes accessed | tf_op | source)
XLA Modules:
  0.0 103.6 jit_solution(13636348723635361189)
XLA Ops:
  7.2 0.7 all-gather.3.cloned.1.call-update
  8.0 0.8 reshape.154
  8.7 0.8 reshape.157
  9.5 0.5 broadcast.141
  10.0 1.3 %reduce.3 = s32[24]{0:T(128)S(1)} reduce(s32[1,24]{1,0:T(1,128)} %param.12, s32[]{:T(128)} %broadcast.141), dimensions={0}, to_apply=%param.12.reduce_sub_computation.3 | reduce | bytes 196 | tf_op args[4]
  11.4 0.7 fusion.15
  12.2 16.8 %all-gather = bf16[8,3,8192]{2,1,0:T(4,128)(2,1)S(1)} all-gather(bf16[1,3,8192]{2,1,0:T(4,128)(2,1)} %bitcast.101), channel_id=1, replica_groups=mesh['dp'=4,'tensor'=8] {'tensor'}, dimensions={0}, use_global_device_ids=true | all-gather | bytes 442368 | tf_op jit(solution)/shard_map/all_gather | solution.py:22
  29.0 0.5 reshape.153
  29.8 0.6 dynamic-slice
  31.1 0.6 gather_fusion.1
  31.8 11.6 %all-gather.3.cloned.1.call-done = bf16[2,24,128,128]{3,2,1,0:T(8,128)(2,1)} async-done(((bf16[2,24,32,128]{3,2,1,0:T(8,128)(2,1)}), bf16[2,24,128,128]{3,2,1,0:T(8,128)(2,1)}) %all-gather.3.cloned.1.call-update) | async-done | bytes 1572880 | tf_op jit(solution)/shard_map/all_gather | solution.py:24
  43.4 2.3 %gather_fusion = bf16[24,2,128,128]{3,2,1,0:T(8,128)(2,1)S(1)} fusion(bf16[2,24,128,128]{3,2,1,0:T(8,128)(2,1)} %all-gather.3.cloned.1.call-done, s32[1024]{0:T(1024)S(1)} %pad_clamp_fusion.1), kind=kCustom, calls=%fused_computation.1 | custom fusion | bytes 3145824 | tf_op jit(solution)/shard_map/jit(_take)/gather | solution.py:25
  46.8 0.5 fusion.1
  47.3 0.4 fusion.9
  47.7 0.6 copy.42
  48.3 0.4 fusion.16
  48.8 0.5 convolution_add_fusion
  49.3 2.0 %fusion = f32[24,2,128,128]{3,2,1,0:T(8,128)} fusion(f32[1,24,128,128]{3,2,0,1:T(8,128)S(1)} %bitcast.95, f32[1,24,128,128]{3,2,0,1:T(8,128)S(1)} %bitcast.94, f32[24]{0:T(128)S(1)} %reshape.162), kind=kLoop, calls=%fused_computation.5 | loop fusion | flops 1572864 | bytes 6291552 | tf_op jit(solution)/shard_map/mul | solution.py:65
  51.3 0.4 broadcast_in_dim.34
  51.7 4.7 %scatter_fusion.1 = f32[2,24,128,128]{3,2,1,0:T(8,128)S(1)} fusion(f32[2,24,128,128]{3,2,1,0:T(8,128)S(1)} %broadcast_in_dim.34, s32[24]{0:T(128)S(1)} %fusion.13, f32[24,2,128,128]{3,2,1,0:T(8,128)} %fusion), kind=kCustom, calls=%fused_computation.3 | custom fusion | bytes 9437280 | tf_op jit(solution)/shard_map/scatter | solution.py:68
  56.4 1.4 %convert_element_type.54 = bf16[2,24,128,128]{3,2,1,0:T(8,128)(2,1)} convert(f32[2,24,128,128]{3,2,1,0:T(8,128)S(1)} %scatter_fusion.1) | non-fusion elementwise | flops 786432 | bytes 4718592 | tf_op jit(solution)/shard_map/convert_element_type | solution.py:70
  57.9 1.9 %scatter_fusion = f32[24,64,128]{2,0,1:T(8,128)S(1)} fusion(f32[24,64,128]{2,0,1:T(8,128)S(1)} %broadcast_in_dim.33, s32[24]{0:T(128)S(1)} %fusion.14, f32[24,24,128]{2,1,0:T(8,128)S(1)} %bitcast.100), kind=kCustom, calls=%fused_computation.2 | custom fusion | flops 73728 | bytes 884832 | tf_op jit(solution)/shard_map/scatter-add | solution.py:51
  59.9 36.2 %all-reduce.2 = bf16[24,8192]{1,0:T(8,128)(2,1)S(1)} all-reduce(f32[24,8192]{1,0:T(8,128)S(1)} %copy_bitcast_fusion), channel_id=2, replica_groups=mesh['dp'=4,'tensor'=8] {'tensor'}, use_global_device_ids=true, to_apply=%region_1.3.clone | all-reduce | flops 196608 | bytes 1179648
  96.0 0.7 dynamic-slice_convert_fusion
  (26 shorter events, 1.8 us)
Async XLA Ops:
  7.2 22.7 %copy-start.2 = (u32[32]{0:T(128)S(1)}, u32[32]{0:T(128)}, u32[]{:S(2)}) copy-start(u32[32]{0:T(128)} %constant.41) | copy-start | bytes 388
  7.2 24.5 %copy-start.1 = (s32[1,24]{1,0:T(1,128)S(1)}, s32[1,24]{1,0:T(1,128)}, u32[]{:S(2)}) copy-start(s32[1,24]{1,0:T(1,128)} %param.12) | copy-start | bytes 292
  7.2 36.2 %all-gather.3.cloned.1.call-start = ((), (), s32[]{:S(2)}) async-start(), calls=%async_computation.1 | async-start | bytes 1966080 | tf_op jit(solution)/shard_map/all_gather | solution.py:24
  7.9 88.8 %reduce-scatter.2.cloned.1.call-start = ((), (), s32[]{:S(2)}) async-start(), calls=%async_computation.2 | async-start | bytes 1966080 | tf_op jit(solution)/shard_map/reduce_scatter | solution.py:69
  45.8 0.7 copy-start
Sparse Core Ops, SparseCore 0:
  9.8 33.5 all-gather.2
  57.9 30.9 reduce-scatter.1
where the time goes:
time: 104 us
  blocking collectives  53 us (51%)
  between operations  14.9 us (14%)
  local copies, waits for them, and re-layouts  13.2 us (13%)
  waiting for transfers between devices  12.3 us (12%)
  other arithmetic  7.79 us (7%)
  matrix products  2.36 us (2%)
    unnamed x1, blocking collectives  36.2 us
    all_gather x1, blocking collectives, body(): gathered = lax.all_gather(tokens, 'tensor', axis=0, tiled=True)  16.8 us
    all_gather x1, waiting for transfers between devices, body(): blocks = lax.all_gather(weight_store, 'dp', axis=2, tiled=True)  11.6 us
    scatter x1, local copies, waits for them, and re-layouts, body(): jnp.zeros_like(partial_value).at[:, block_home[0]].set(partial_value)  4.69 us
    gather x2, local copies, waits for them, and re-layouts, body(): ordered = jnp.take(blocks, block_home[0], axis=1)  2.36 us
  transfers between devices with their start and end apart: 2, of which 1 were waited for; matrix products, arithmetic and copies ran while one was open for 9% of the time, Pallas kernels for 0%

commit v1 on v0

v1 whole, which is shorter than its diff:
```python
import functools
import jax
import jax.numpy as jnp
from jax import lax
from jax.experimental import pallas as pl
from jax.experimental.pallas import tpu as pltpu
from jax.sharding import PartitionSpec as P

MESH = pl.DeviceIdType.MESH
F32 = jnp.float32
BF16 = jnp.bfloat16
LANES = 128


def exchange_kernel(
    n_dp, n_t, cols_s, count_s, home_s, cols_v, tok_ref, w_ref, gh_ref,
    hid_ref, wg_ref, cr_ref, ca_ref,
    tq, x, xt, wb, ps, pr, ga, cf, c,
    s1, r1, s2, r2, sc, rc, sp, rp, sg, rg, st, rt, loc,
):
    n_dev = n_dp * n_t
    me_n, me_t = lax.axis_index("dp"), lax.axis_index("tensor")
    me = me_n * n_t + me_t
    own, blocks, _ = tok_ref.shape
    rows = w_ref.shape[2]
    blk = w_ref.shape[3]
    hb, kmax = cols_s.shape
    groups = LANES // rows
    tiles = blocks // groups
    tokens = own * n_dev
    group_rows = own * n_t
    span = kmax * rows

    barrier = pltpu.get_barrier_semaphore()

    def greet(i, carry):
        o = lax.rem(me + i, n_dev)
        pl.semaphore_signal(barrier, inc=1, device_id=(o // n_t, lax.rem(o, n_t)), device_id_type=MESH)
        return carry

    lax.fori_loop(1, n_dev, greet, 0)

    tok = tok_ref[...].astype(F32)
    for n in range(n_dp):
        tq[n] = jnp.concatenate(
            [tok[:, g * tiles:(g + 1) * tiles, n * rows:(n + 1) * rows] for g in range(groups)], axis=2
        ).astype(BF16)
    for h in range(hb):
        for m in range(2):
            parts = []
            for k in range(kmax):
                keep = jnp.where(k < count_s[h], 1.0, 0.0).astype(F32)
                parts.append(w_ref[m, home_s[0, h * kmax + k]].astype(F32) * keep)
            wb[h, :, m * blk:(m + 1) * blk] = jnp.concatenate(parts, axis=0).astype(BF16)
    pl.semaphore_wait(barrier, n_dev - 1)

    own_tok = pltpu.make_async_copy(tq.at[me_n], x.at[me_n, me_t], loc.at[0])
    own_tok.start()
    own_cols = pltpu.make_async_copy(cols_v, ca_ref.at[me_t], loc.at[1])
    own_cols.start()

    def first(d):
        n = lax.rem(me_n + d, n_dp)
        return pltpu.make_async_remote_copy(
            src_ref=tq.at[n], dst_ref=x.at[me_n, me_t], send_sem=s1.at[d], recv_sem=r1.at[d],
            device_id=(n, me_t), device_id_type=MESH)

    def second(e):
        t = lax.rem(me_t + e, n_t)
        return pltpu.make_async_remote_copy(
            src_ref=x.at[:, me_t], dst_ref=x.at[:, me_t], send_sem=s2.at[e], recv_sem=r2.at[e],
            device_id=(me_n, t), device_id_type=MESH)

    def columns(e):
        t = lax.rem(me_t + e, n_t)
        return pltpu.make_async_remote_copy(
            src_ref=cols_v, dst_ref=ca_ref.at[me_t], send_sem=sc.at[e], recv_sem=rc.at[e],
            device_id=(me_n, t), device_id_type=MESH)

    def partial(d):
        n = lax.rem(me_n + d, n_dp)
        return pltpu.make_async_remote_copy(
            src_ref=ps.at[n], dst_ref=pr.at[d], send_sem=sp.at[d], recv_sem=rp.at[d],
            device_id=(n, me_t), device_id_type=MESH)

    def grads(d):
        n = lax.rem(me_n + d, n_dp)
        return pltpu.make_async_remote_copy(
            src_ref=ga.at[me_n], dst_ref=ga.at[me_n], send_sem=sg.at[d], recv_sem=rg.at[d],
            device_id=(n, me_t), device_id_type=MESH)

    def terms(i):
        o = lax.rem(me + i, n_dev)
        n, t = o // n_t, lax.rem(o, n_t)
        return pltpu.make_async_remote_copy(
            src_ref=c.at[n, t], dst_ref=cr_ref.at[me_n, me_t], send_sem=st.at[i], recv_sem=rt.at[i],
            device_id=(n, t), device_id_type=MESH)

    def each(count, act):
        lax.fori_loop(1, count, lambda i, carry: (act(i), carry)[1], 0)

    each(n_dp, lambda d: first(d).start())
    each(n_t, lambda e: columns(e).start())
    own_tok.wait()
    each(n_dp, lambda d: first(d).wait_recv())
    each(n_t, lambda e: second(e).start())
    each(n_t, lambda e: second(e).wait_recv())

    flat = x[...].reshape(tokens, tiles, LANES).astype(F32)
    turned = jnp.swapaxes(flat, 0, 1)
    for j in range(tiles):
        upright = turned[j].T
        for g in range(groups):
            xt[g * tiles + j] = upright[g * rows:(g + 1) * rows]

    picked, mine = [], []
    for h in range(hb):
        chosen = jnp.concatenate([xt[cols_s[h, k]] for k in range(kmax)], axis=0).astype(BF16)
        picked.append(chosen)
        pre = lax.dot_general(chosen, wb[h], (((0,), (0,)), ((), ())), preferred_element_type=F32)
        for n in range(n_dp):
            ps[n, :, h * 2 * blk:(h + 1) * 2 * blk] = pre[n * group_rows:(n + 1) * group_rows].astype(BF16)
    each(n_dp, lambda d: partial(d).start())
    total = ps[me_n].astype(F32)
    each(n_dp, lambda d: partial(d).wait_recv())
    for d in range(1, n_dp):
        total = total + pr[d].astype(F32)
    grad_parts = []
    for h in range(hb):
        gate = total[:, h * 2 * blk:(h * 2 + 1) * blk]
        up = total[:, (h * 2 + 1) * blk:(h + 1) * 2 * blk]
        grad_in = gh_ref[:, h * blk:(h + 1) * blk].astype(F32)
        sigma = jax.nn.sigmoid(gate)
        act = gate * sigma
        hid_ref[:, h * blk:(h + 1) * blk] = (act * up).astype(BF16)
        grad_parts += [grad_in * up * sigma * (1.0 + gate * (1.0 - sigma)), grad_in * act]
    ga[me_n] = jnp.concatenate(grad_parts, axis=1).astype(BF16)
    each(n_dp, lambda d: grads(d).start())
    each(n_dp, lambda d: grads(d).wait_recv())

    every = jnp.concatenate([ga[n].astype(F32) for n in range(n_dp)], axis=0).astype(BF16)
    for h in range(hb):
        cf[:, h * span:(h + 1) * span] = lax.dot_general(
            every[:, h * 2 * blk:(h + 1) * 2 * blk], wb[h], (((1,), (1,)), ((), ())), preferred_element_type=F32)
    for n in range(n_dp):
        part = cf[n * group_rows:(n + 1) * group_rows, :]
        for t in range(n_t):
            c[n, t] = part[t * own:(t + 1) * own].astype(BF16)
    own_terms = pltpu.make_async_copy(c.at[me_n, me_t], cr_ref.at[me_n, me_t], loc.at[2])
    own_terms.start()
    each(n_dev, lambda i: terms(i).start())

    for h in range(hb):
        grown = jnp.dot(picked[h], every[:, h * 2 * blk:(h + 1) * 2 * blk], preferred_element_type=F32)
        for k in range(kmax):
            keep = jnp.where(k < count_s[h], 1.0, 0.0).astype(F32)
            for m in range(2):
                wg_ref[m, h * kmax + k] = (
                    grown[k * rows:(k + 1) * rows, m * blk:(m + 1) * blk] * keep).astype(BF16)

    own_cols.wait()
    own_terms.wait()
    each(n_dev, lambda i: terms(i).wait_recv())
    each(n_t, lambda e: columns(e).wait_recv())
    each(n_dp, lambda d: first(d).wait_send())
    each(n_t, lambda e: second(e).wait_send())
    each(n_t, lambda e: columns(e).wait_send())
    each(n_dp, lambda d: partial(d).wait_send())
    each(n_dp, lambda d: grads(d).wait_send())
    each(n_dev, lambda i: terms(i).wait_send())


def place_kernel(cr_ref, ca_s, home_s, hid_in, wg_in, hid_ref, gt_ref, gw_ref, acc):
    n_dp, n_t, own, _ = cr_ref.shape
    rows, blk = wg_in.shape[2:]
    slots = wg_in.shape[1]
    kmax = ca_s.shape[2]
    blocks = acc.shape[0]
    hid_ref[...] = hid_in[...]
    for s in range(slots):
        spot = home_s[0, s]
        for m in range(2):
            gw_ref[m, spot] = wg_in[m, s]
    acc[...] = jnp.zeros_like(acc)

    def group(t, carry):
        sources = [cr_ref[n, t].astype(F32) for n in range(n_dp)]
        for s in range(slots):
            col = ca_s[t, s // kmax, s % kmax]
            acc[col] += jnp.concatenate([v[:, s * rows:(s + 1) * rows] for v in sources], axis=1)
        return carry

    lax.fori_loop(0, n_t, group, 0)
    for b in range(blocks):
        gt_ref[:, b * blk:(b + 1) * blk] = acc[b].astype(BF16)


def body(n_dp, n_t, tokens, weight_store, block_cols, block_count, block_home, grad_hidden):
    own, width = tokens.shape
    _, slots, rows, blk = weight_store.shape
    blocks = width // blk
    hb, kmax = block_cols.shape
    n_dev = n_dp * n_t
    group_rows = own * n_t
    groups = LANES // rows
    tiles = blocks // groups
    ff = hb * blk
    vmem = pl.BlockSpec(memory_space=pltpu.VMEM)
    smem = pl.BlockSpec(memory_space=pltpu.SMEM)
    dma = pltpu.SemaphoreType.DMA
    hid, wg, cr, ca = pl.pallas_call(
        functools.partial(exchange_kernel, n_dp, n_t),
        out_shape=(
            jax.ShapeDtypeStruct((group_rows, ff), BF16),
            jax.ShapeDtypeStruct((2, slots, rows, blk), BF16),
            jax.ShapeDtypeStruct((n_dp, n_t, own, slots * rows), BF16),
            jax.ShapeDtypeStruct((n_t, hb, kmax), jnp.int32),
        ),
        in_specs=[smem, smem, smem, vmem, vmem, vmem, vmem],
        out_specs=(vmem, vmem, vmem, vmem),
        scratch_shapes=[
            pltpu.VMEM((n_dp, own, tiles, LANES), BF16),
            pltpu.VMEM((n_dp, n_t, own, tiles, LANES), BF16),
            pltpu.VMEM((blocks, rows, own * n_dev), F32),
            pltpu.VMEM((hb, kmax * rows, 2 * blk), BF16),
            pltpu.VMEM((n_dp, group_rows, 2 * ff), BF16),
            pltpu.VMEM((n_dp, group_rows, 2 * ff), BF16),
            pltpu.VMEM((n_dp, group_rows, 2 * ff), BF16),
            pltpu.VMEM((own * n_dev, slots * rows), F32),
            pltpu.VMEM((n_dp, n_t, own, slots * rows), BF16),
            dma((n_dp,)), dma((n_dp,)), dma((n_t,)), dma((n_t,)), dma((n_t,)), dma((n_t,)),
            dma((n_dp,)), dma((n_dp,)), dma((n_dp,)), dma((n_dp,)), dma((n_dev,)), dma((n_dev,)),
            dma((3,)),
        ],
        compiler_params=pltpu.CompilerParams(
            collective_id=0, has_side_effects=True, vmem_limit_bytes=56 * 1024 * 1024),
        name="exchange",
    )(block_cols, block_count, block_home, block_cols, tokens.reshape(own, blocks, blk), weight_store, grad_hidden)
    return pl.pallas_call(
        place_kernel,
        out_shape=(
            jax.ShapeDtypeStruct((group_rows, ff), BF16),
            jax.ShapeDtypeStruct((own, width), BF16),
            jax.ShapeDtypeStruct((2, slots, rows, blk), BF16),
        ),
        in_specs=[vmem, smem, smem, vmem, vmem],
        out_specs=(vmem, vmem, vmem),
        scratch_shapes=[pltpu.VMEM((blocks, own, LANES), F32)],
        compiler_params=pltpu.CompilerParams(vmem_limit_bytes=32 * 1024 * 1024),
        name="place",
    )(cr, ca, block_home, hid, wg)


def solution(mesh):
    return jax.shard_map(
        functools.partial(body, mesh.shape["dp"], mesh.shape["tensor"]),
        mesh=mesh,
        in_specs=(
            P(("dp", "tensor"), None),
            P(None, "tensor", "dp", None),
            P("tensor", None),
            P("tensor"),
            P("tensor", None),
            P("dp", "tensor"),
        ),
        out_specs=(P("dp", "tensor"), P(("dp", "tensor"), None), P(None, "tensor", "dp", None)),
        check_vma=False,
    )
```

time: 104 us -> 45.6 us (0.44)
  blocking collectives: 53 us -> 0 us
  Pallas kernels: 0 us -> 39.1 us
  between operations: 14.9 us -> 0.65 us
  waiting for transfers between devices: 12.3 us -> 0 us
  other arithmetic: 7.79 us -> 0 us
  local copies, waits for them, and re-layouts: 13.2 us -> 5.48 us
  matrix products: 2.36 us -> 0 us
    pallas_call x0 -> x2, Pallas kernels: none -> 39.1 us  [the longest x1 36.1 us: body(): pl.pallas_call(functools.partial(exchange_kernel, n_dp, n_t), out_shape=(...]
    unnamed x1 -> x0, blocking collectives: 36.2 us -> none
    all_gather x1 -> x0, blocking collectives: 16.8 us -> none  [body(): gathered = lax.all_gather(tokens, 'tensor', axis=0, tiled=True)]
    all_gather x1 -> x0, waiting for transfers between devices: 11.6 us -> none  [body(): blocks = lax.all_gather(weight_store, 'dp', axis=2, tiled=True)]
    scatter x1 -> x0, local copies, waits for them, and re-layouts: 4.69 us -> none  [body(): jnp.zeros_like(partial_value).at[:, block_home[0]].set(partial_value)]
    unnamed x8 -> x11, local copies, waits for them, and re-layouts: 1.33 us -> 5.48 us
    reshape x6 -> x0, local copies, waits for them, and re-layouts: 2.98 us -> none  [the longest x2 1.53 us: body(): flat_cols = block_cols.reshape(-1)]
    gather x3 -> x0, local copies, waits for them, and re-layouts: 2.95 us -> none  [the longest x2 2.36 us: body(): ordered = jnp.take(blocks, block_home[0], axis=1)]
  transfers between devices with their start and end apart: 2 -> 0, of which waited for: 1 -> 0; matrix products, arithmetic and copies ran while one was open for 9% -> 0% of each run, Pallas kernels for 0% -> 0%
where the time goes in v1:
time: 45.6 us; the launch traced here: 45.2 us
  Pallas kernels  39.1 us (86%)
  local copies, waits for them, and re-layouts  5.48 us (12%)
  between operations  0.65 us (1%)
    pallas_call x1, Pallas kernels, body(): pl.pallas_call(functools.partial(exchange_kernel, n_dp, n_t), out_shape=(...  36.1 us
    unnamed x11, local copies, waits for them, and re-layouts  5.48 us
    pallas_call x1, Pallas kernels, body(): pl.pallas_call(place_kernel, out_shape=(jax.ShapeDtypeStruct((group_rows,...  2.98 us

profile of v1, /device:TPU:0, one launch (start us, length us, event | category | flops | bytes accessed | tf_op | source)
XLA Modules:
  0.0 45.2 jit_solution(9186915151249667499)
XLA Ops:
  0.6 1.5 %copy.11 = bf16[1,3,64,128]{3,2,1,0:T(8,128)(2,1)} copy(bf16[1,3,64,128]{3,1,2,0:T(4,128)(2,1)} %bitcast.5) | data formatting | bytes 98304
  2.1 36.1 %exchange.1 = (bf16[24,384]{1,0:T(8,128)(2,1)}, bf16[2,24,32,128]{3,2,1,0:T(8,128)(2,1)}, bf16[4,8,3,768]{3,2,1,0:T(4,128)(2,1)}, s32[8,3,8]{2,1,0:T(4,128)}) custom-call(s32[3,8]{1,0:T(4,128)} %cols_v.1, s32[3]{0:T(128)} %count_s.1, s32[1,24]{1,0:T(1,128)} %home_s.3, s32[3,8]{1,0:T(4,128)} %cols_v.1, bf16[3,64,128]{2,1,0:T(8,128)(2,1)} %bitcast.4, ...), custom_call_target="tpu_custom_call" | custom-call | tf_op jit(solution)/shard_map/exchange/pallas_call | solution.py:211
  38.2 0.0 copy-start.4
  38.2 0.6 %copy-done.4 = s32[1,24]{1,0:T(1,128)S(1)} copy-done((s32[1,24]{1,0:T(1,128)S(1)}, s32[1,24]{1,0:T(1,128)}, u32[]{:S(2)}) %copy-start.4) | copy-done | bytes 120
  38.8 0.0 copy-start
  38.9 1.0 %copy-done = bf16[2,24,32,128]{3,2,1,0:T(8,128)(2,1)S(1)} copy-done((bf16[2,24,32,128]{3,2,1,0:T(8,128)(2,1)S(1)}, bf16[2,24,32,128]{3,2,1,0:T(8,128)(2,1)}, u32[]{:S(2)}) %copy-start) | copy-done | bytes 393240
  39.8 0.0 copy-start.1
  39.8 0.9 %copy-done.1 = bf16[4,8,3,768]{3,2,1,0:T(4,128)(2,1)S(1)} copy-done((bf16[4,8,3,768]{3,2,1,0:T(4,128)(2,1)S(1)}, bf16[4,8,3,768]{3,2,1,0:T(4,128)(2,1)}, u32[]{:S(2)}) %copy-start.1) | copy-done | bytes 147480
  40.8 0.0 copy-start.2
  40.8 0.7 %copy-done.2 = bf16[24,384]{1,0:T(8,128)(2,1)S(1)} copy-done((bf16[24,384]{1,0:T(8,128)(2,1)S(1)}, bf16[24,384]{1,0:T(8,128)(2,1)}, u32[]{:S(2)}) %copy-start.2) | copy-done | bytes 18456
  41.5 0.0 copy-start.3
  41.5 0.7 %copy-done.3 = s32[8,3,8]{2,1,0:T(4,128)S(1)} copy-done((s32[8,3,8]{2,1,0:T(4,128)S(1)}, s32[8,3,8]{2,1,0:T(4,128)}, u32[]{:S(2)}) %copy-start.3) | copy-done | bytes 792
  42.2 3.0 %place.1 = (bf16[24,384]{1,0:T(8,128)(2,1)}, bf16[3,8192]{1,0:T(4,128)(2,1)}, bf16[2,24,32,128]{3,2,1,0:T(8,128)(2,1)}) custom-call(bf16[4,8,3,768]{3,2,1,0:T(4,128)(2,1)S(1)} %copy-done.1, s32[8,3,8]{2,1,0:T(4,128)S(1)} %copy-done.3, s32[1,24]{1,0:T(1,128)S(1)} %copy-done.4, bf16[24,384]{1,0:T(8,128)(2,1)S(1)} %copy-done.2, bf16[2,24,32,128]{3,2,1,0:T(8,128)(2,1)S(1)} %copy-done), custom_call_target="tpu_custom_call" | custom-call | tf_op jit(solution)/shard_map/place/pallas_call | solution.py:239
Async XLA Ops:
  38.2 0.7 %copy-start.4 = (s32[1,24]{1,0:T(1,128)S(1)}, s32[1,24]{1,0:T(1,128)}, u32[]{:S(2)}) copy-start(s32[1,24]{1,0:T(1,128)} %home_s.3) | copy-start | bytes 292
  38.8 1.0 %copy-start = (bf16[2,24,32,128]{3,2,1,0:T(8,128)(2,1)S(1)}, bf16[2,24,32,128]{3,2,1,0:T(8,128)(2,1)}, u32[]{:S(2)}) copy-start(bf16[2,24,32,128]{3,2,1,0:T(8,128)(2,1)} %get-tuple-element.10.wg_in) | copy-start | bytes 1179652
  39.8 0.9 %copy-start.1 = (bf16[4,8,3,768]{3,2,1,0:T(4,128)(2,1)S(1)}, bf16[4,8,3,768]{3,2,1,0:T(4,128)(2,1)}, u32[]{:S(2)}) copy-start(bf16[4,8,3,768]{3,2,1,0:T(4,128)(2,1)} %get-tuple-element.7.cr_ref) | copy-start | bytes 442372
  40.8 0.7 %copy-start.2 = (bf16[24,384]{1,0:T(8,128)(2,1)S(1)}, bf16[24,384]{1,0:T(8,128)(2,1)}, u32[]{:S(2)}) copy-start(bf16[24,384]{1,0:T(8,128)(2,1)} %get-tuple-element.9.hid_in) | copy-start | bytes 55300
  41.5 0.7 %copy-start.3 = (s32[8,3,8]{2,1,0:T(4,128)S(1)}, s32[8,3,8]{2,1,0:T(4,128)}, u32[]{:S(2)}) copy-start(s32[8,3,8]{2,1,0:T(4,128)} %get-tuple-element.8.ca_s) | copy-start | bytes 2308

commit v2 on v1

v2 whole, which is shorter than its diff:
```python
import functools
import jax
import jax.numpy as jnp
from jax import lax
from jax.experimental import pallas as pl
from jax.experimental.pallas import tpu as pltpu
from jax.sharding import PartitionSpec as P

MESH = pl.DeviceIdType.MESH
F32 = jnp.float32
BF16 = jnp.bfloat16
LANES = 128


def exchange_kernel(
    n_dp, n_t, cols_s, count_s, home_s, cols_v, tok_ref, w_hbm, gh_ref,
    hid_out, wg_out, cr_ref, ca_ref,
    wv, tq, x, xt, wb, ps, pr, ga, c, hid_ref, wg_ref,
    s1, r1, s2, r2, sc, rc, sp, rp, sg, rg, st, rt, loc,
):
    n_dev = n_dp * n_t
    me_n, me_t = lax.axis_index("dp"), lax.axis_index("tensor")
    me = me_n * n_t + me_t
    own, width = tok_ref.shape
    rows = w_hbm.shape[2]
    blk = w_hbm.shape[3]
    blocks = width // blk
    hb, kmax = cols_s.shape
    groups = LANES // rows
    tiles = blocks // groups
    tokens = own * n_dev
    group_rows = own * n_t
    span = kmax * rows

    barrier = pltpu.get_barrier_semaphore()

    def greet(i, carry):
        o = lax.rem(me + i, n_dev)
        pl.semaphore_signal(barrier, inc=1, device_id=(o // n_t, lax.rem(o, n_t)), device_id_type=MESH)
        return carry

    lax.fori_loop(1, n_dev, greet, 0)
    fetch = pltpu.make_async_copy(w_hbm, wv, loc.at[0])
    fetch.start()

    flat_tok = tok_ref[...].astype(F32)
    tok = jnp.stack([flat_tok[:, b * blk:(b + 1) * blk] for b in range(blocks)], axis=1)
    for n in range(n_dp):
        tq[n] = jnp.concatenate(
            [tok[:, g * tiles:(g + 1) * tiles, n * rows:(n + 1) * rows] for g in range(groups)], axis=2
        ).astype(BF16)
    fetch.wait()
    for h in range(hb):
        for m in range(2):
            parts = []
            for k in range(kmax):
                keep = jnp.where(k < count_s[h], 1.0, 0.0).astype(F32)
                parts.append(wv[m, home_s[0, h * kmax + k]].astype(F32) * keep)
            wb[h, :, m * blk:(m + 1) * blk] = jnp.concatenate(parts, axis=0).astype(BF16)
    pl.semaphore_wait(barrier, n_dev - 1)

    def ahead(d):
        return lax.rem(me_n + d, n_dp)

    def behind(d):
        return lax.rem(me_n - d + n_dp, n_dp)

    def first(d):
        n = ahead(d)
        return pltpu.make_async_remote_copy(
            src_ref=tq.at[n], dst_ref=x.at[me_n, me_t], send_sem=s1.at[d], recv_sem=r1.at[d],
            device_id=(n, me_t), device_id_type=MESH)

    def second(d, e):
        n, t = behind(d), lax.rem(me_t + e, n_t)
        return pltpu.make_async_remote_copy(
            src_ref=x.at[n, me_t], dst_ref=x.at[n, me_t], send_sem=s2.at[d, e], recv_sem=r2.at[d, e],
            device_id=(me_n, t), device_id_type=MESH)

    def columns(e):
        t = lax.rem(me_t + e, n_t)
        return pltpu.make_async_remote_copy(
            src_ref=cols_v, dst_ref=ca_ref.at[me_t], send_sem=sc.at[e], recv_sem=rc.at[e],
            device_id=(me_n, t), device_id_type=MESH)

    def partial(h, d):
        n = ahead(d)
        return pltpu.make_async_remote_copy(
            src_ref=ps.at[h, n], dst_ref=pr.at[h, d], send_sem=sp.at[h, d], recv_sem=rp.at[h, d],
            device_id=(n, me_t), device_id_type=MESH)

    def grads(h, d):
        n = ahead(d)
        return pltpu.make_async_remote_copy(
            src_ref=ga.at[h, me_n], dst_ref=ga.at[h, me_n], send_sem=sg.at[h, d], recv_sem=rg.at[h, d],
            device_id=(n, me_t), device_id_type=MESH)

    def terms(d, e):
        n, t = behind(d), lax.rem(me_t + e, n_t)
        return pltpu.make_async_remote_copy(
            src_ref=c.at[n, t], dst_ref=cr_ref.at[me_n, me_t], send_sem=st.at[d, e], recv_sem=rt.at[d, e],
            device_id=(n, t), device_id_type=MESH)

    def each(count, act, start=1):
        lax.fori_loop(start, count, lambda i, carry: (act(i), carry)[1], 0)

    each(n_dp, lambda d: first(d).start())
    own_tok = pltpu.make_async_copy(tq.at[me_n], x.at[me_n, me_t], loc.at[0])
    own_tok.start()
    own_cols = pltpu.make_async_copy(cols_v, ca_ref.at[me_t], loc.at[1])
    own_cols.start()
    own_tok.wait()
    each(n_t, lambda e: second(0, e).start())

    def relay(d):
        first(d).wait_recv()
        each(n_t, lambda e: second(d, e).start())

    each(n_dp, relay)
    each(n_t, lambda e: columns(e).start())
    each(n_dp, lambda d: each(n_t, lambda e: second(d, e).wait_recv()), 0)

    flat = x[...].reshape(tokens, tiles, LANES).astype(F32)
    turned = jnp.swapaxes(flat, 0, 1)
    for j in range(tiles):
        upright = turned[j].T
        for g in range(groups):
            xt[g * tiles + j] = upright[g * rows:(g + 1) * rows]

    picked = []
    for h in range(hb):
        chosen = jnp.concatenate([xt[cols_s[h, k]] for k in range(kmax)], axis=0).astype(BF16)
        picked.append(chosen)
        pre = lax.dot_general(chosen, wb[h], (((0,), (0,)), ((), ())), preferred_element_type=F32)
        for n in range(n_dp):
            ps[h, n] = pre[n * group_rows:(n + 1) * group_rows].astype(BF16)
        each(n_dp, lambda d: partial(h, d).start())
    for h in range(hb):
        total = ps[h, me_n].astype(F32)
        each(n_dp, lambda d: partial(h, d).wait_recv())
        for d in range(1, n_dp):
            total = total + pr[h, d].astype(F32)
        gate, up = total[:, :blk], total[:, blk:]
        grad_in = gh_ref[:, h * blk:(h + 1) * blk].astype(F32)
        sigma = jax.nn.sigmoid(gate)
        act = gate * sigma
        hid_ref[:, h * blk:(h + 1) * blk] = (act * up).astype(BF16)
        ga[h, me_n] = jnp.concatenate(
            [grad_in * up * sigma * (1.0 + gate * (1.0 - sigma)), grad_in * act], axis=1).astype(BF16)
        each(n_dp, lambda d: grads(h, d).start())
    hid_copy = pltpu.make_async_copy(hid_ref, hid_out, loc.at[0])
    hid_copy.start()

    def send_terms(n):
        part = jnp.concatenate([
            lax.dot_general(ga[h, n], wb[h], (((1,), (1,)), ((), ())), preferred_element_type=F32)
            for h in range(hb)], axis=1)
        for t in range(n_t):
            c[n, t] = part[t * own:(t + 1) * own].astype(BF16)

    send_terms(me_n)
    own_terms = pltpu.make_async_copy(c.at[me_n, me_t], cr_ref.at[me_n, me_t], loc.at[2])
    own_terms.start()
    each(n_t, lambda e: terms(0, e).start())

    def others(d):
        for h in range(hb):
            grads(h, d).wait_recv()
        send_terms(behind(d))
        each(n_t, lambda e: terms(d, e).start(), 0)

    each(n_dp, others)

    for h in range(hb):
        every = jnp.concatenate([ga[h, n].astype(F32) for n in range(n_dp)], axis=0).astype(BF16)
        grown = jnp.dot(picked[h], every, preferred_element_type=F32)
        for k in range(kmax):
            keep = jnp.where(k < count_s[h], 1.0, 0.0).astype(F32)
            for m in range(2):
                wg_ref[m, h * kmax + k] = (
                    grown[k * rows:(k + 1) * rows, m * blk:(m + 1) * blk] * keep).astype(BF16)
    wg_copy = pltpu.make_async_copy(wg_ref, wg_out, loc.at[3])
    wg_copy.start()

    own_cols.wait()
    own_terms.wait()
    hid_copy.wait()
    each(n_t, lambda e: terms(0, e).wait_recv())
    each(n_dp, lambda d: each(n_t, lambda e: terms(d, e).wait_recv(), 0))
    each(n_t, lambda e: columns(e).wait_recv())
    each(n_dp, lambda d: first(d).wait_send())
    each(n_dp, lambda d: each(n_t, lambda e: second(d, e).wait_send()), 0)
    each(n_t, lambda e: columns(e).wait_send())
    for h in range(hb):
        each(n_dp, lambda d: partial(h, d).wait_send())
        each(n_dp, lambda d: grads(h, d).wait_send())
    each(n_t, lambda e: terms(0, e).wait_send())
    each(n_dp, lambda d: each(n_t, lambda e: terms(d, e).wait_send(), 0))
    wg_copy.wait()


def place_kernel(cr_ref, ca_s, home_s, hid_in, wg_in, hid_ref, gt_ref, gw_out, acc, wv, fetched, sent):
    n_dp, n_t, own, _ = cr_ref.shape
    rows, blk = wg_in.shape[2:]
    slots = wg_in.shape[1]
    kmax = ca_s.shape[2]
    blocks = acc.shape[0]

    def fetch(s):
        return pltpu.make_async_copy(wg_in.at[:, s], wv.at[:, home_s[0, s]], fetched.at[s])

    for s in range(slots):
        fetch(s).start()
    hid_ref[...] = hid_in[...]
    acc[...] = jnp.zeros_like(acc)
    for s in range(slots):
        fetch(s).wait()
    put = pltpu.make_async_copy(wv, gw_out, sent)
    put.start()

    def group(t, carry):
        sources = [cr_ref[n, t].astype(F32) for n in range(n_dp)]
        for s in range(slots):
            col = ca_s[t, s // kmax, s % kmax]
            acc[col] += jnp.concatenate([v[:, s * rows:(s + 1) * rows] for v in sources], axis=1)
        return carry

    lax.fori_loop(0, n_t, group, 0)
    for b in range(blocks):
        gt_ref[:, b * blk:(b + 1) * blk] = acc[b].astype(BF16)
    put.wait()


def body(n_dp, n_t, tokens, weight_store, block_cols, block_count, block_home, grad_hidden):
    own, width = tokens.shape
    _, slots, rows, blk = weight_store.shape
    blocks = width // blk
    hb, kmax = block_cols.shape
    n_dev = n_dp * n_t
    group_rows = own * n_t
    groups = LANES // rows
    tiles = blocks // groups
    ff = hb * blk
    vmem = pl.BlockSpec(memory_space=pltpu.VMEM)
    smem = pl.BlockSpec(memory_space=pltpu.SMEM)
    place = pl.BlockSpec(memory_space=pl.ANY)
    dma = pltpu.SemaphoreType.DMA
    hid, wg, cr, ca = pl.pallas_call(
        functools.partial(exchange_kernel, n_dp, n_t),
        out_shape=(
            jax.ShapeDtypeStruct((group_rows, ff), BF16),
            jax.ShapeDtypeStruct((2, slots, rows, blk), BF16),
            jax.ShapeDtypeStruct((n_dp, n_t, own, slots * rows), BF16),
            jax.ShapeDtypeStruct((n_t, hb, kmax), jnp.int32),
        ),
        in_specs=[smem, smem, smem, vmem, vmem, place, vmem],
        out_specs=(place, place, place, place),
        scratch_shapes=[
            pltpu.VMEM((2, slots, rows, blk), BF16),
            pltpu.VMEM((n_dp, own, tiles, LANES), BF16),
            pltpu.VMEM((n_dp, n_t, own, tiles, LANES), BF16),
            pltpu.VMEM((blocks, rows, own * n_dev), F32),
            pltpu.VMEM((hb, kmax * rows, 2 * blk), BF16),
            pltpu.VMEM((hb, n_dp, group_rows, 2 * blk), BF16),
            pltpu.VMEM((hb, n_dp, group_rows, 2 * blk), BF16),
            pltpu.VMEM((hb, n_dp, group_rows, 2 * blk), BF16),
            pltpu.VMEM((n_dp, n_t, own, slots * rows), BF16),
            pltpu.VMEM((group_rows, ff), BF16),
            pltpu.VMEM((2, slots, rows, blk), BF16),
            dma((n_dp,)), dma((n_dp,)), dma((n_dp, n_t)), dma((n_dp, n_t)), dma((n_t,)), dma((n_t,)),
            dma((hb, n_dp)), dma((hb, n_dp)), dma((hb, n_dp)), dma((hb, n_dp)), dma((n_dp, n_t)), dma((n_dp, n_t)),
            dma((4,)),
        ],
        compiler_params=pltpu.CompilerParams(
            collective_id=0, has_side_effects=True, vmem_limit_bytes=60 * 1024 * 1024),
        name="exchange",
    )(block_cols, block_count, block_home, block_cols, tokens, weight_store, grad_hidden)
    return pl.pallas_call(
        place_kernel,
        out_shape=(
            jax.ShapeDtypeStruct((group_rows, ff), BF16),
            jax.ShapeDtypeStruct((own, width), BF16),
            jax.ShapeDtypeStruct((2, slots, rows, blk), BF16),
        ),
        in_specs=[vmem, smem, smem, vmem, place],
        out_specs=(vmem, vmem, place),
        scratch_shapes=[
            pltpu.VMEM((blocks, own, LANES), F32),
            pltpu.VMEM((2, slots, rows, blk), BF16),
            dma((slots,)), dma(()),
        ],
        compiler_params=pltpu.CompilerParams(vmem_limit_bytes=60 * 1024 * 1024),
        name="place",
    )(cr, ca, block_home, hid, wg)


def solution(mesh):
    return jax.shard_map(
        functools.partial(body, mesh.shape["dp"], mesh.shape["tensor"]),
        mesh=mesh,
        in_specs=(
            P(("dp", "tensor"), None),
            P(None, "tensor", "dp", None),
            P("tensor", None),
            P("tensor"),
            P("tensor", None),
            P("dp", "tensor"),
        ),
        out_specs=(P("dp", "tensor"), P(("dp", "tensor"), None), P(None, "tensor", "dp", None)),
        check_vma=False,
    )
```

time: 45.6 us -> 39.1 us (0.86)
  local copies, waits for them, and re-layouts: 5.48 us -> 0 us
  Pallas kernels: 39.1 us -> 38.1 us
    unnamed x11 -> x0, local copies, waits for them, and re-layouts: 5.48 us -> none
    pallas_call x1, Pallas kernels: 36.1 us -> 33.9 us  [body(): pl.pallas_call(functools.partial(exchange_kernel, n_dp, n_t), out_shape=(...]
    pallas_call x1, Pallas kernels: 2.98 us -> 4.24 us  [body(): pl.pallas_call(place_kernel, out_shape=(jax.ShapeDtypeStruct((group_rows,...]
where the time goes in v2:
time: 39.1 us; the launch traced here: 38.8 us
  Pallas kernels  38.1 us (97%)
  between operations  0.64 us (2%)
    pallas_call x1, Pallas kernels, body(): pl.pallas_call(functools.partial(exchange_kernel, n_dp, n_t), out_shape=(...  33.9 us
    pallas_call x1, Pallas kernels, body(): pl.pallas_call(place_kernel, out_shape=(jax.ShapeDtypeStruct((group_rows,...  4.24 us

profile of v2, /device:TPU:0, one launch (start us, length us, event | category | flops | bytes accessed | tf_op | source)
XLA Modules:
  0.0 38.8 jit_solution(5359726390816611738)
XLA Ops:
  0.6 33.9 %exchange.1 = (bf16[24,384]{1,0:T(8,128)(2,1)}, bf16[2,24,32,128]{3,2,1,0:T(8,128)(2,1)}, bf16[4,8,3,768]{3,2,1,0:T(4,128)(2,1)}, s32[8,3,8]{2,1,0:T(4,128)}) custom-call(s32[3,8]{1,0:T(4,128)} %cols_v.1, s32[3]{0:T(128)} %count_s.1, s32[1,24]{1,0:T(1,128)} %home_s.3, s32[3,8]{1,0:T(4,128)} %cols_v.1, bf16[3,8192]{1,0:T(4,128)(2,1)} %tok_ref.1, ...), custom_call_target="tpu_custom_call" | custom-call | tf_op jit(solution)/shard_map/exchange/pallas_call | solution.py:248
  34.5 4.2 %place.1 = (bf16[24,384]{1,0:T(8,128)(2,1)}, bf16[3,8192]{1,0:T(4,128)(2,1)}, bf16[2,24,32,128]{3,2,1,0:T(8,128)(2,1)}) custom-call(bf16[4,8,3,768]{3,2,1,0:T(4,128)(2,1)} %get-tuple-element.7.cr_ref, s32[8,3,8]{2,1,0:T(4,128)} %get-tuple-element.8.ca_s, s32[1,24]{1,0:T(1,128)} %home_s.3, bf16[24,384]{1,0:T(8,128)(2,1)} %get-tuple-element.9.hid_in, ...), custom_call_target="tpu_custom_call" | custom-call | tf_op jit(solution)/shard_map/place/pallas_call | solution.py:278

commit v3 on v2

--- a/solution.py
+++ b/solution.py
@@ -13,10 +13,11 @@
 
 
 def exchange_kernel(
-    n_dp, n_t, cols_s, count_s, home_s, cols_v, tok_ref, w_hbm, gh_ref,
+    n_dp, n_t, cols_in, count_in, home_in, tok_in, w_hbm, gh_in,
     hid_out, wg_out, cr_ref, ca_ref,
+    cols_s, count_s, home_s, cols_v, tok_ref, gh_ref,
     wv, tq, x, xt, wb, ps, pr, ga, c, hid_ref, wg_ref,
-    s1, r1, s2, r2, sc, rc, sp, rp, sg, rg, st, rt, loc,
+    s1, r1, s2, r2, sf, rf, sc, rc, sp, rp, sg, rg, st, rt, loc,
 ):
     n_dev = n_dp * n_t
     me_n, me_t = lax.axis_index("dp"), lax.axis_index("tensor")
@@ -34,14 +35,23 @@
 
     barrier = pltpu.get_barrier_semaphore()
 
-    def greet(i, carry):
-        o = lax.rem(me + i, n_dev)
-        pl.semaphore_signal(barrier, inc=1, device_id=(o // n_t, lax.rem(o, n_t)), device_id_type=MESH)
-        return carry
-
-    lax.fori_loop(1, n_dev, greet, 0)
-    fetch = pltpu.make_async_copy(w_hbm, wv, loc.at[0])
-    fetch.start()
+    def greet(n, t):
+        pl.semaphore_signal(barrier, inc=1, device_id=(n, t), device_id_type=MESH)
+
+    def each(count, act, start=1):
+        lax.fori_loop(start, count, lambda i, carry: (act(i), carry)[1], 0)
+
+    each(n_t, lambda e: greet(me_n, lax.rem(me_t + e, n_t)))
+    each(n_dp, lambda d: greet(lax.rem(me_n + d, n_dp), me_t))
+    fetches = [
+        pltpu.make_async_copy(src, dst, loc.at[4 + i])
+        for i, (src, dst) in enumerate((
+            (tok_in, tok_ref), (w_hbm, wv), (cols_in, cols_s), (count_in, count_s),
+            (home_in, home_s), (cols_in, cols_v), (gh_in, gh_ref)))
+    ]
+    for fetch in fetches:
+        fetch.start()
+    fetches[0].wait()
 
     flat_tok = tok_ref[...].astype(F32)
     tok = jnp.stack([flat_tok[:, b * blk:(b + 1) * blk] for b in range(blocks)], axis=1)
@@ -49,7 +59,8 @@
         tq[n] = jnp.concatenate(
             [tok[:, g * tiles:(g + 1) * tiles, n * rows:(n + 1) * rows] for g in range(groups)], axis=2
         ).astype(BF16)
-    fetch.wait()
+    for fetch in fetches[1:]:
+        fetch.wait()
     for h in range(hb):
         for m in range(2):
             parts = []
@@ -57,7 +68,10 @@
                 keep = jnp.where(k < count_s[h], 1.0, 0.0).astype(F32)
                 parts.append(wv[m, home_s[0, h * kmax + k]].astype(F32) * keep)
             wb[h, :, m * blk:(m + 1) * blk] = jnp.concatenate(parts, axis=0).astype(BF16)
-    pl.semaphore_wait(barrier, n_dev - 1)
+    pl.semaphore_wait(barrier, n_dp + n_t - 2)
+
+    chips = n_t // 2
+    partner = me_t + 1 - 2 * lax.rem(me_t, 2)
 
     def ahead(d):
         return lax.rem(me_n + d, n_dp)
@@ -72,11 +86,17 @@
             device_id=(n, me_t), device_id_type=MESH)
 
     def second(d, e):
-        n, t = behind(d), lax.rem(me_t + e, n_t)
+        n, t = behind(d), lax.rem(me_t + 2 * e, n_t)
         return pltpu.make_async_remote_copy(
             src_ref=x.at[n, me_t], dst_ref=x.at[n, me_t], send_sem=s2.at[d, e], recv_sem=r2.at[d, e],
             device_id=(me_n, t), device_id_type=MESH)
 
+    def share(d, e):
+        n, t = behind(d), lax.rem(me_t - 2 * e + n_t, n_t)
+        return pltpu.make_async_remote_copy(
+            src_ref=x.at[n, t], dst_ref=x.at[n, t], send_sem=sf.at[d, e], recv_sem=rf.at[d, e],
+            device_id=(me_n, partner), device_id_type=MESH)
+
     def columns(e):
         t = lax.rem(me_t + e, n_t)
         return pltpu.make_async_remote_copy(
@@ -100,9 +120,6 @@
         return pltpu.make_async_remote_copy(
             src_ref=c.at[n, t], dst_ref=cr_ref.at[me_n, me_t], send_sem=st.at[d, e], recv_sem=rt.at[d, e],
             device_id=(n, t), device_id_type=MESH)
-
-    def each(count, act, start=1):
-        lax.fori_loop(start, count, lambda i, carry: (act(i), carry)[1], 0)
 
     each(n_dp, lambda d: first(d).start())
     own_tok = pltpu.make_async_copy(tq.at[me_n], x.at[me_n, me_t], loc.at[0])
@@ -110,15 +127,23 @@
     own_cols = pltpu.make_async_copy(cols_v, ca_ref.at[me_t], loc.at[1])
     own_cols.start()
     own_tok.wait()
-    each(n_t, lambda e: second(0, e).start())
 
     def relay(d):
-        first(d).wait_recv()
-        each(n_t, lambda e: second(d, e).start())
-
-    each(n_dp, relay)
+        each(chips, lambda e: second(d, e).start())
+        share(d, 0).start()
+
+    relay(0)
+    each(n_dp, lambda d: (first(d).wait_recv(), relay(d)))
     each(n_t, lambda e: columns(e).start())
-    each(n_dp, lambda d: each(n_t, lambda e: second(d, e).wait_recv()), 0)
+
+    def pass_on(d):
+        def one(e):
+            second(d, e).wait_recv()
+            share(d, e).start()
+        each(chips, one)
+
+    each(n_dp, pass_on, 0)
+    each(n_dp, lambda d: each(chips, lambda e: share(d, e).wait_recv(), 0), 0)
 
     flat = x[...].reshape(tokens, tiles, LANES).astype(F32)
     turned = jnp.swapaxes(flat, 0, 1)
@@ -151,12 +176,18 @@
     hid_copy = pltpu.make_async_copy(hid_ref, hid_out, loc.at[0])
     hid_copy.start()
 
+    wide = -(-hb * span // LANES)
+
     def send_terms(n):
-        part = jnp.concatenate([
+        parts = [
             lax.dot_general(ga[h, n], wb[h], (((1,), (1,)), ((), ())), preferred_element_type=F32)
-            for h in range(hb)], axis=1)
+            for h in range(hb)]
+        if wide * LANES > hb * span:
+            parts.append(jnp.zeros((group_rows, wide * LANES - hb * span), F32))
+        part = jnp.concatenate(parts, axis=1)
         for t in range(n_t):
-            c[n, t] = part[t * own:(t + 1) * own].astype(BF16)
+            c[n, t] = jnp.concatenate([
+                part[t * own:(t + 1) * own, j * LANES:(j + 1) * LANES] for j in range(wide)], axis=0).astype(BF16)
 
     send_terms(me_n)
     own_terms = pltpu.make_async_copy(c.at[me_n, me_t], cr_ref.at[me_n, me_t], loc.at[2])
@@ -189,7 +220,8 @@
     each(n_dp, lambda d: each(n_t, lambda e: terms(d, e).wait_recv(), 0))
     each(n_t, lambda e: columns(e).wait_recv())
     each(n_dp, lambda d: first(d).wait_send())
-    each(n_dp, lambda d: each(n_t, lambda e: second(d, e).wait_send()), 0)
+    each(n_dp, lambda d: each(chips, lambda e: second(d, e).wait_send()), 0)
+    each(n_dp, lambda d: each(chips, lambda e: share(d, e).wait_send(), 0), 0)
     each(n_t, lambda e: columns(e).wait_send())
     for h in range(hb):
         each(n_dp, lambda d: partial(h, d).wait_send())
@@ -199,35 +231,50 @@
     wg_copy.wait()
 
 
-def place_kernel(cr_ref, ca_s, home_s, hid_in, wg_in, hid_ref, gt_ref, gw_out, acc, wv, fetched, sent):
-    n_dp, n_t, own, _ = cr_ref.shape
+def place_kernel(cr_in, ca_s, home_s, hid_in, wg_in, hid_out, gt_ref, gw_out, acc, cr_ref, hid_ref, wv, fetched, other):
+    n_dp, n_t, packed, _ = cr_in.shape
     rows, blk = wg_in.shape[2:]
     slots = wg_in.shape[1]
-    kmax = ca_s.shape[2]
-    blocks = acc.shape[0]
+    hb, kmax = ca_s.shape[1:]
+    blocks, own, _ = acc.shape
+    groups = LANES // rows
 
     def fetch(s):
         return pltpu.make_async_copy(wg_in.at[:, s], wv.at[:, home_s[0, s]], fetched.at[s])
 
+    cr_copy = pltpu.make_async_copy(cr_in, cr_ref, other.at[0])
+    cr_copy.start()
+    hid_copy = pltpu.make_async_copy(hid_in, hid_ref, other.at[1])
+    hid_copy.start()
     for s in range(slots):
         fetch(s).start()
-    hid_ref[...] = hid_in[...]
     acc[...] = jnp.zeros_like(acc)
+
+    def group(t, carry):
+        sources = [cr_ref[n, t].astype(F32) for n in range(n_dp)]
+        mixed = [
+            jnp.concatenate([v[:, g * rows:(g + 1) * rows] for v in sources], axis=1) for g in range(groups)]
+        for h in range(hb):
+            cols = [ca_s[t, h, k] for k in range(kmax)]
+            held = [acc[col] for col in cols]
+            for k in range(kmax):
+                j, g = (h * kmax + k) // groups, (h * kmax + k) % groups
+                acc[cols[k]] = held[k] + mixed[g][j * own:(j + 1) * own]
+        return carry
+
+    cr_copy.wait()
+    lax.fori_loop(0, n_t // 2, group, 0)
+    hid_copy.wait()
+    hid_put = pltpu.make_async_copy(hid_ref, hid_out, other.at[2])
+    hid_put.start()
     for s in range(slots):
         fetch(s).wait()
-    put = pltpu.make_async_copy(wv, gw_out, sent)
+    put = pltpu.make_async_copy(wv, gw_out, other.at[3])
     put.start()
-
-    def group(t, carry):
-        sources = [cr_ref[n, t].astype(F32) for n in range(n_dp)]
-        for s in range(slots):
-            col = ca_s[t, s // kmax, s % kmax]
-            acc[col] += jnp.concatenate([v[:, s * rows:(s + 1) * rows] for v in sources], axis=1)
-        return carry
-
-    lax.fori_loop(0, n_t, group, 0)
+    lax.fori_loop(n_t // 2, n_t, group, 0)
     for b in range(blocks):
         gt_ref[:, b * blk:(b + 1) * blk] = acc[b].astype(BF16)
+    hid_put.wait()
     put.wait()
 
 
@@ -241,6 +288,7 @@
     groups = LANES // rows
     tiles = blocks // groups
     ff = hb * blk
+    packed = own * -(-slots * rows // LANES)
     vmem = pl.BlockSpec(memory_space=pltpu.VMEM)
     smem = pl.BlockSpec(memory_space=pltpu.SMEM)
     place = pl.BlockSpec(memory_space=pl.ANY)
@@ -250,12 +298,18 @@
         out_shape=(
             jax.ShapeDtypeStruct((group_rows, ff), BF16),
             jax.ShapeDtypeStruct((2, slots, rows, blk), BF16),
-            jax.ShapeDtypeStruct((n_dp, n_t, own, slots * rows), BF16),
+            jax.ShapeDtypeStruct((n_dp, n_t, packed, LANES), BF16),
             jax.ShapeDtypeStruct((n_t, hb, kmax), jnp.int32),
         ),
-        in_specs=[smem, smem, smem, vmem, vmem, place, vmem],
+        in_specs=[place] * 6,
         out_specs=(place, place, place, place),
         scratch_shapes=[
+            pltpu.SMEM((hb, kmax), jnp.int32),
+            pltpu.SMEM((hb,), jnp.int32),
+            pltpu.SMEM((1, slots), jnp.int32),
+            pltpu.VMEM((hb, kmax), jnp.int32),
+            pltpu.VMEM((own, width), BF16),
+            pltpu.VMEM((group_rows, ff), BF16),
             pltpu.VMEM((2, slots, rows, blk), BF16),
             pltpu.VMEM((n_dp, own, tiles, LANES), BF16),
             pltpu.VMEM((n_dp, n_t, own, tiles, LANES), BF16),
@@ -264,17 +318,18 @@
             pltpu.VMEM((hb, n_dp, group_rows, 2 * blk), BF16),
             pltpu.VMEM((hb, n_dp, group_rows, 2 * blk), BF16),
             pltpu.VMEM((hb, n_dp, group_rows, 2 * blk), BF16),
-            pltpu.VMEM((n_dp, n_t, own, slots * rows), BF16),
+            pltpu.VMEM((n_dp, n_t, packed, LANES), BF16),
             pltpu.VMEM((group_rows, ff), BF16),
             pltpu.VMEM((2, slots, rows, blk), BF16),
-            dma((n_dp,)), dma((n_dp,)), dma((n_dp, n_t)), dma((n_dp, n_t)), dma((n_t,)), dma((n_t,)),
+            dma((n_dp,)), dma((n_dp,)), dma((n_dp, n_t // 2)), dma((n_dp, n_t // 2)),
+            dma((n_dp, n_t // 2)), dma((n_dp, n_t // 2)), dma((n_t,)), dma((n_t,)),
             dma((hb, n_dp)), dma((hb, n_dp)), dma((hb, n_dp)), dma((hb, n_dp)), dma((n_dp, n_t)), dma((n_dp, n_t)),
-            dma((4,)),
+            dma((11,)),
         ],
         compiler_params=pltpu.CompilerParams(
             collective_id=0, has_side_effects=True, vmem_limit_bytes=60 * 1024 * 1024),
         name="exchange",
-    )(block_cols, block_count, block_home, block_cols, tokens, weight_store, grad_hidden)
+    )(block_cols, block_count, block_home, tokens, weight_store, grad_hidden)
     return pl.pallas_call(
         place_kernel,
         out_shape=(
@@ -282,12 +337,14 @@
             jax.ShapeDtypeStruct((own, width), BF16),
             jax.ShapeDtypeStruct((2, slots, rows, blk), BF16),
         ),
-        in_specs=[vmem, smem, smem, vmem, place],
-        out_specs=(vmem, vmem, place),
+        in_specs=[place, smem, smem, place, place],
+        out_specs=(place, vmem, place),
         scratch_shapes=[
             pltpu.VMEM((blocks, own, LANES), F32),
+            pltpu.VMEM((n_dp, n_t, packed, LANES), BF16),
+            pltpu.VMEM((group_rows, ff), BF16),
             pltpu.VMEM((2, slots, rows, blk), BF16),
-            dma((slots,)), dma(()),
+            dma((slots,)), dma((4,)),
         ],
         compiler_params=pltpu.CompilerParams(vmem_limit_bytes=60 * 1024 * 1024),
         name="place",

time: 39.1 us -> 35.4 us (0.905)
  Pallas kernels: 38.1 us -> 34.5 us
    pallas_call x1, Pallas kernels: 33.9 us -> 30.4 us  [body(): pl.pallas_call(functools.partial(exchange_kernel, n_dp, n_t), out_shape=(...]
where the time goes in v3:
time: 35.4 us; the launch traced here: 35.1 us
  Pallas kernels  34.5 us (97%)
  between operations  0.64 us (2%)
    pallas_call x1, Pallas kernels, body(): pl.pallas_call(functools.partial(exchange_kernel, n_dp, n_t), out_shape=(...  30.4 us
    pallas_call x1, Pallas kernels, body(): pl.pallas_call(place_kernel, out_shape=(jax.ShapeDtypeStruct((group_rows,...  4.16 us

profile of v3, /device:TPU:0, one launch (start us, length us, event | category | flops | bytes accessed | tf_op | source)
XLA Modules:
  0.0 35.1 jit_solution(18211295076288981882)
XLA Ops:
  0.6 30.4 %exchange.1 = (bf16[24,384]{1,0:T(8,128)(2,1)}, bf16[2,24,32,128]{3,2,1,0:T(8,128)(2,1)}, bf16[4,8,18,128]{3,2,1,0:T(8,128)(2,1)}, s32[8,3,8]{2,1,0:T(4,128)}) custom-call(s32[3,8]{1,0:T(4,128)} %cols_in.1, s32[3]{0:T(128)} %count_in.1, s32[1,24]{1,0:T(1,128)} %home_s.1, bf16[3,8192]{1,0:T(4,128)(2,1)} %tok_in.1, bf16[2,24,32,128]{3,2,1,0:T(8,128)(2,1)} %w_hbm.1, ...), custom_call_target="tpu_custom_call" | custom-call | tf_op jit(solution)/shard_map/exchange/pallas_call | solution.py:296
  31.0 4.2 %place.1 = (bf16[24,384]{1,0:T(8,128)(2,1)}, bf16[3,8192]{1,0:T(4,128)(2,1)}, bf16[2,24,32,128]{3,2,1,0:T(8,128)(2,1)}) custom-call(bf16[4,8,18,128]{3,2,1,0:T(8,128)(2,1)} %get-tuple-element.7.cr_in, s32[8,3,8]{2,1,0:T(4,128)} %get-tuple-element.8.ca_s, s32[1,24]{1,0:T(1,128)} %home_s.1, bf16[24,384]{1,0:T(8,128)(2,1)} %get-tuple-element.9.hid_in, ...), custom_call_target="tpu_custom_call" | custom-call | tf_op jit(solution)/shard_map/place/pallas_call | solution.py:333

commit v4 on v3

--- a/solution.py
+++ b/solution.py
@@ -73,11 +73,20 @@
     chips = n_t // 2
     partner = me_t + 1 - 2 * lax.rem(me_t, 2)
 
+    def paired(d):
+        if n_dp & (n_dp - 1):
+            return lax.rem(me_n + d, n_dp), lax.rem(me_n - d + n_dp, n_dp)
+        mate, bit = 0, 1
+        while bit < n_dp:
+            mate += lax.rem(me_n // bit + d // bit, 2) * bit
+            bit *= 2
+        return mate, mate
+
     def ahead(d):
-        return lax.rem(me_n + d, n_dp)
+        return paired(d)[0]
 
     def behind(d):
-        return lax.rem(me_n - d + n_dp, n_dp)
+        return paired(d)[1]
 
     def first(d):
         n = ahead(d)
@@ -231,7 +240,10 @@
     wg_copy.wait()
 
 
-def place_kernel(cr_in, ca_s, home_s, hid_in, wg_in, hid_out, gt_ref, gw_out, acc, cr_ref, hid_ref, wv, fetched, other):
+def place_kernel(
+    cr_in, ca_in, home_in, hid_in, wg_in, hid_out, gt_ref, gw_out,
+    acc, cr_ref, hid_ref, wv, ca_s, home_s, fetched, other,
+):
     n_dp, n_t, packed, _ = cr_in.shape
     rows, blk = wg_in.shape[2:]
     slots = wg_in.shape[1]
@@ -242,13 +254,18 @@
     def fetch(s):
         return pltpu.make_async_copy(wg_in.at[:, s], wv.at[:, home_s[0, s]], fetched.at[s])
 
+    home_copy = pltpu.make_async_copy(home_in, home_s, other.at[4])
+    home_copy.start()
+    ca_copy = pltpu.make_async_copy(ca_in, ca_s, other.at[5])
+    ca_copy.start()
     cr_copy = pltpu.make_async_copy(cr_in, cr_ref, other.at[0])
     cr_copy.start()
     hid_copy = pltpu.make_async_copy(hid_in, hid_ref, other.at[1])
     hid_copy.start()
+    acc[...] = jnp.zeros_like(acc)
+    home_copy.wait()
     for s in range(slots):
         fetch(s).start()
-    acc[...] = jnp.zeros_like(acc)
 
     def group(t, carry):
         sources = [cr_ref[n, t].astype(F32) for n in range(n_dp)]
@@ -262,6 +279,7 @@
                 acc[cols[k]] = held[k] + mixed[g][j * own:(j + 1) * own]
         return carry
 
+    ca_copy.wait()
     cr_copy.wait()
     lax.fori_loop(0, n_t // 2, group, 0)
     hid_copy.wait()
@@ -290,7 +308,6 @@
     ff = hb * blk
     packed = own * -(-slots * rows // LANES)
     vmem = pl.BlockSpec(memory_space=pltpu.VMEM)
-    smem = pl.BlockSpec(memory_space=pltpu.SMEM)
     place = pl.BlockSpec(memory_space=pl.ANY)
     dma = pltpu.SemaphoreType.DMA
     hid, wg, cr, ca = pl.pallas_call(
@@ -337,14 +354,16 @@
             jax.ShapeDtypeStruct((own, width), BF16),
             jax.ShapeDtypeStruct((2, slots, rows, blk), BF16),
         ),
-        in_specs=[place, smem, smem, place, place],
+        in_specs=[place] * 5,
         out_specs=(place, vmem, place),
         scratch_shapes=[
             pltpu.VMEM((blocks, own, LANES), F32),
             pltpu.VMEM((n_dp, n_t, packed, LANES), BF16),
             pltpu.VMEM((group_rows, ff), BF16),
             pltpu.VMEM((2, slots, rows, blk), BF16),
-            dma((slots,)), dma((4,)),
+            pltpu.SMEM((n_t, hb, kmax), jnp.int32),
+            pltpu.SMEM((1, slots), jnp.int32),
+            dma((slots,)), dma((6,)),
         ],
         compiler_params=pltpu.CompilerParams(vmem_limit_bytes=60 * 1024 * 1024),
         name="place",

time: 35.4 us -> 34 us (0.960)
  Pallas kernels: 34.5 us -> 33.1 us
    pallas_call x1, Pallas kernels: 4.16 us -> 3.28 us  [body(): pl.pallas_call(place_kernel, out_shape=(jax.ShapeDtypeStruct((group_rows,...]
    pallas_call x1, Pallas kernels: 30.4 us -> 29.9 us  [body(): pl.pallas_call(functools.partial(exchange_kernel, n_dp, n_t), out_shape=(...]
where the time goes in v4:
time: 34 us; the launch traced here: 33.8 us
  Pallas kernels  33.1 us (97%)
  between operations  0.64 us (2%)
    pallas_call x1, Pallas kernels, body(): pl.pallas_call(functools.partial(exchange_kernel, n_dp, n_t), out_shape=(...  29.9 us
    pallas_call x1, Pallas kernels, body(): pl.pallas_call(place_kernel, out_shape=(jax.ShapeDtypeStruct((group_rows,...  3.28 us

profile of v4, /device:TPU:0, one launch (start us, length us, event | category | flops | bytes accessed | tf_op | source)
XLA Modules:
  0.0 33.8 jit_solution(15480739797349544601)
XLA Ops:
  0.6 29.9 %exchange.1 = (bf16[24,384]{1,0:T(8,128)(2,1)}, bf16[2,24,32,128]{3,2,1,0:T(8,128)(2,1)}, bf16[4,8,18,128]{3,2,1,0:T(8,128)(2,1)}, s32[8,3,8]{2,1,0:T(4,128)}) custom-call(s32[3,8]{1,0:T(4,128)} %cols_in.1, s32[3]{0:T(128)} %count_in.1, s32[1,24]{1,0:T(1,128)} %home_in.3, bf16[3,8192]{1,0:T(4,128)(2,1)} %tok_in.1, bf16[2,24,32,128]{3,2,1,0:T(8,128)(2,1)} %w_hbm.1, ...), custom_call_target="tpu_custom_call" | custom-call | tf_op jit(solution)/shard_map/exchange/pallas_call | solution.py:313
  30.5 3.3 %place.1 = (bf16[24,384]{1,0:T(8,128)(2,1)}, bf16[3,8192]{1,0:T(4,128)(2,1)}, bf16[2,24,32,128]{3,2,1,0:T(8,128)(2,1)}) custom-call(bf16[4,8,18,128]{3,2,1,0:T(8,128)(2,1)} %get-tuple-element.7.cr_in, s32[8,3,8]{2,1,0:T(4,128)} %get-tuple-element.8.ca_in, s32[1,24]{1,0:T(1,128)} %home_in.3, bf16[24,384]{1,0:T(8,128)(2,1)} %get-tuple-element.9.hid_in, ...), custom_call_target="tpu_custom_call" | custom-call | tf_op jit(solution)/shard_map/place/pallas_call | solution.py:350

commit v5 on v4

--- a/solution.py
+++ b/solution.py
@@ -225,8 +225,6 @@
     own_cols.wait()
     own_terms.wait()
     hid_copy.wait()
-    each(n_t, lambda e: terms(0, e).wait_recv())
-    each(n_dp, lambda d: each(n_t, lambda e: terms(d, e).wait_recv(), 0))
     each(n_t, lambda e: columns(e).wait_recv())
     each(n_dp, lambda d: first(d).wait_send())
     each(n_dp, lambda d: each(chips, lambda e: second(d, e).wait_send()), 0)
@@ -238,6 +236,8 @@
     each(n_t, lambda e: terms(0, e).wait_send())
     each(n_dp, lambda d: each(n_t, lambda e: terms(d, e).wait_send(), 0))
     wg_copy.wait()
+    each(n_t, lambda e: terms(0, e).wait_recv())
+    each(n_dp, lambda d: each(n_t, lambda e: terms(d, e).wait_recv(), 0))
 
 
 def place_kernel(

time: 34 us -> 33.4 us (0.982)
  Pallas kernels: 33.1 us -> 32.5 us
    pallas_call x1, Pallas kernels: 29.9 us -> 29.2 us  [body(): pl.pallas_call(functools.partial(exchange_kernel, n_dp, n_t), out_shape=(...]
where the time goes in v5:
time: 33.4 us; the launch traced here: 33.1 us
  Pallas kernels  32.5 us (97%)
  between operations  0.64 us (2%)
    pallas_call x1, Pallas kernels, body(): pl.pallas_call(functools.partial(exchange_kernel, n_dp, n_t), out_shape=(...  29.2 us
    pallas_call x1, Pallas kernels, body(): pl.pallas_call(place_kernel, out_shape=(jax.ShapeDtypeStruct((group_rows,...  3.28 us

profile of v5, /device:TPU:0, one launch (start us, length us, event | category | flops | bytes accessed | tf_op | source)
XLA Modules:
  0.0 33.1 jit_solution(10835686130553551629)
XLA Ops:
  0.6 29.2 %exchange.1 = (bf16[24,384]{1,0:T(8,128)(2,1)}, bf16[2,24,32,128]{3,2,1,0:T(8,128)(2,1)}, bf16[4,8,18,128]{3,2,1,0:T(8,128)(2,1)}, s32[8,3,8]{2,1,0:T(4,128)}) custom-call(s32[3,8]{1,0:T(4,128)} %cols_in.1, s32[3]{0:T(128)} %count_in.1, s32[1,24]{1,0:T(1,128)} %home_in.3, bf16[3,8192]{1,0:T(4,128)(2,1)} %tok_in.1, bf16[2,24,32,128]{3,2,1,0:T(8,128)(2,1)} %w_hbm.1, ...), custom_call_target="tpu_custom_call" | custom-call | tf_op jit(solution)/shard_map/exchange/pallas_call | solution.py:313
  29.9 3.3 %place.1 = (bf16[24,384]{1,0:T(8,128)(2,1)}, bf16[3,8192]{1,0:T(4,128)(2,1)}, bf16[2,24,32,128]{3,2,1,0:T(8,128)(2,1)}) custom-call(bf16[4,8,18,128]{3,2,1,0:T(8,128)(2,1)} %get-tuple-element.7.cr_in, s32[8,3,8]{2,1,0:T(4,128)} %get-tuple-element.8.ca_in, s32[1,24]{1,0:T(1,128)} %home_in.3, bf16[24,384]{1,0:T(8,128)(2,1)} %get-tuple-element.9.hid_in, ...), custom_call_target="tpu_custom_call" | custom-call | tf_op jit(solution)/shard_map/place/pallas_call | solution.py:350
